TPU v7x, 256 devices: a whole 4x4x8 slice. The times are simulated.
256 devices in a mesh: visit: 32 (over z_lo, y, core), tile: 8 (over z_hi, x).
Axes of the slice: x: 4, y: 4, z: 8 (z_hi: 2, z_lo: 4; z = z_hi * 4 + z_lo), core: 2. Of those that a mesh axis runs over, the one named last changes fastest.
Arguments:
- exposures: float32 [32, 2048, 256], P('visit', 'tile'), may hold values from 0.3 to 3
- sky_model: float32 [2048, 256], P(('tile', 'visit')), may hold values from 0.5 to 2
- blur_kernels: float32 [32, 31, 31], P('visit'), may hold values from 0.05 to 1
- coverage: int32 [32, 8], P('visit'), may hold values from 0 to 1, as said below
Outputs:
- deconvolved: float32 [2048, 256], P(('tile', 'visit'))
Inputs may be any that keep to these rules, and one draw needn't show every extreme that they name: `coverage`: every tile is covered by at least one exposure.
All inputs are finite; a program needn't handle non-finite values.
Results may differ from a plain program's by a relative error of at most 0.0001.
Values sent between devices are 32-bit elements; how exact they have to be, the bound alone decides.
A program may use at most 128 MiB of HBM per device.

v0:
```python
import jax
import jax.numpy as jnp
from jax import lax
from jax.sharding import PartitionSpec as P

ITERS = 2


def padded(array, sides, width):
    for axis, dim in sides:
        peers, length = (lax.axis_size(axis), array.shape[dim])
        up = [(i, (i + 1) % peers) for i in range(peers - 1)]
        down = [(j, i) for i, j in up]
        last = lax.slice_in_dim(array, length - width, length, axis=dim)
        initial = lax.slice_in_dim(array, 0, width, axis=dim)
        before = lax.ppermute(last, axis, up)
        after = lax.ppermute(initial, axis, down)
        array = jnp.concatenate([before, array, after], axis=dim)
    return array


def band_lookup(width, kernel_len):
    half = kernel_len // 2
    differ = jnp.arange(width)[:, None] - jnp.arange(width)[None, :] + half
    band_table = (differ[:, :, None] == jnp.arange(kernel_len)[None, None, :]).astype(jnp.float32)
    return band_table.reshape(width * width, kernel_len)


def column_operator(kernel, band_table, width):
    kernel_len = kernel.shape[0]
    operator = jnp.dot(band_table, kernel.T, precision=lax.Precision.HIGHEST)
    operator = operator.reshape(width, width, kernel_len).transpose(0, 2, 1)
    return operator.reshape(width, kernel_len * width)


def correlate(extended, operator):
    width = operator.shape[0]
    kernel_len = operator.shape[1] // width
    out_rows = extended.shape[0] - (kernel_len - 1)
    product = jnp.dot(extended, operator, precision=lax.Precision.HIGHEST)
    product = product.reshape(extended.shape[0], kernel_len, width)
    total = product[0:out_rows, 0]
    for offset in range(1, kernel_len):
        total = total + product[offset : offset + out_rows, offset]
    return total


def body(exposures, sky_model, blur_kernels, coverage):
    tile_rows = exposures.shape[1]
    tile_cols = exposures.shape[2]
    kernel_len = blur_kernels.shape[1]
    radius = kernel_len // 2
    tile_count = lax.axis_size("tile")
    tile_place = lax.axis_index("tile")
    kernels = blur_kernels / jnp.sum(blur_kernels, axis=(1, 2), keepdims=True)
    band_table = band_lookup(tile_cols, kernel_len)
    forward_ops = [column_operator(kernels[0], band_table, tile_cols)]
    flipped_ops = [column_operator(kernels[0][::-1, ::-1], band_table, tile_cols)]
    global_row = tile_place * tile_rows - radius + jnp.arange(tile_rows + 2 * radius)
    row_owner = jnp.floor_divide(global_row, tile_rows)
    selector = (row_owner[:, None] == jnp.arange(tile_count)[None, :]).astype(jnp.float32)
    weight_rows = jnp.dot(coverage.astype(jnp.float32), selector.T, precision=lax.Precision.HIGHEST)
    own_weights = weight_rows[:, radius : radius + tile_rows]
    member = 0
    column_sums = forward_ops[member].reshape(tile_cols, kernel_len, tile_cols).sum(axis=0)
    row_window = jnp.stack(
        [weight_rows[member][offset : offset + tile_rows] for offset in range(kernel_len)], axis=1
    )
    norm_local = jnp.dot(row_window, column_sums, precision=lax.Precision.HIGHEST)
    norm_shard = lax.psum_scatter(norm_local, "visit", scatter_dimension=0, tiled=True)
    model_shard = sky_model
    for step in range(ITERS):
        whole = lax.all_gather(model_shard, "visit", axis=0, tiled=True)
        model_wide = padded(whole, (("tile", 0),), radius)
        member = 0
        blurred = correlate(model_wide, flipped_ops[member])
        ratio_list = [own_weights[member][:, None] * exposures[member] / blurred]
        ratios = jnp.stack(ratio_list)
        ratio_wide = padded(ratios, (("tile", 1),), radius)
        member = 0
        numerator = correlate(ratio_wide[member], forward_ops[member])
        update = lax.psum_scatter(numerator, "visit", scatter_dimension=0, tiled=True)
        model_shard = model_shard * update / norm_shard
    return model_shard


def solution(mesh):
    return jax.shard_map(
        body,
        mesh=mesh,
        in_specs=(
            P("visit", "tile", None),
            P(("tile", "visit"), None),
            P("visit", None, None),
            P("visit", None),
        ),
        out_specs=P(("tile", "visit"), None),
        check_vma=False,
    )
```

profile of v0, /device:TPU:2, one launch (start us, length us, event | category | flops | bytes accessed | tf_op | source)
XLA Modules:
  0.0 643.0 jit_solution(17559654957804409515)
XLA Ops:
  6.5 45.5 %all_gather.6 = f32[256,256]{1,0:T(8,128)S(1)} all-gather(f32[8,256]{1,0:T(8,128)} %param.5), channel_id=1, replica_groups=mesh['visit'=32,'tile'=8] {'visit'}, dimensions={0}, use_global_device_ids=true | all-gather | bytes 270336 | tf_op jit(solution)/shard_map/all_gather | solution.py:73
  52.1 3.4 collective-permute-start
  55.5 2.4 collective-permute-start.1
  58.0 1.4 reduce_sum.18
  59.3 1.4 broadcast_divide_fusion
  60.8 0.9 fusion.116
  61.8 6.3 fusion.117
  68.2 6.1 fusion.17
  74.4 10.0 %copy.7 = f32[256,31,256]{0,2,1:T(8,128)} copy(f32[256,31,256]{2,1,0:T(8,128)} %fusion.17) | data formatting | bytes 16252928 | tf_op jit(solution)/shard_map/transpose | solution.py:32
  84.5 11.2 %fusion.10 = f32[286,31,256]{2,0,1:T(8,128)S(1)} fusion(f32[256,31,256]{0,2,1:T(8,128)} %copy.7, f32[15,256]{1,0:T(8,128)S(1)} %collective-permute-done.1, f32[256,256]{1,0:T(8,128)S(1)} %all_gather.6, f32[15,256]{1,0:T(8,128)S(1)} %collective-permute-done), kind=kOutput, calls=%fused_computation.11 | convolution fusion | flops 6972652544 | bytes 17498112 | tf_op jit(solution)/shard_map/dot_general | solution.py:40
  95.7 0.8 fusion.81
  96.5 3.4 collective-permute-start.2
  99.9 2.4 collective-permute-start.3
  102.4 1.1 fusion.118
  103.8 9.9 %copy.8 = f32[256,31,256]{0,2,1:T(8,128)} copy(f32[256,31,256]{2,1,0:T(8,128)} %get-tuple-element.47) | data formatting | bytes 16252928 | tf_op jit(solution)/shard_map/transpose | solution.py:32
  113.7 11.2 %fusion.6 = f32[286,31,256]{2,0,1:T(8,128)S(1)} fusion(f32[256,31,256]{0,2,1:T(8,128)} %copy.8, f32[1,15,256]{2,1,0:T(8,128)S(1)} %collective-permute-done.3, f32[1,256,256]{2,1,0:T(8,128)S(1)} %fusion.81, f32[1,15,256]{2,1,0:T(8,128)S(1)} %collective-permute-done.2), kind=kOutput, calls=%fused_computation.7 | convolution fusion | flops 6972652544 | bytes 17498112 | tf_op jit(solution)/shard_map/dot_general | solution.py:40
  124.9 1.4 fusion.65
  126.4 130.0 %reduce-scatter.6.cloned.1.call-done = f32[8,256]{1,0:T(8,128)} async-done(((f32[256,256]{1,0:T(8,128)}), f32[8,256]{1,0:T(8,128)}) %reduce-scatter.6.cloned.1.call-update) | async-done | bytes 8208 | tf_op jit(solution)/shard_map/reduce_scatter | solution.py:70
  256.4 144.5 %reduce-scatter.4.cloned.1.call-done = f32[8,256]{1,0:T(8,128)} async-done(((f32[256,256]{1,0:T(8,128)}), f32[8,256]{1,0:T(8,128)}) %reduce-scatter.4.cloned.1.call-update) | async-done | bytes 8208 | tf_op jit(solution)/shard_map/reduce_scatter | solution.py:82
  401.6 38.3 %all_gather.7 = f32[256,256]{1,0:T(8,128)S(1)} all-gather(f32[8,256]{1,0:T(8,128)S(1)} %multiply_divide_fusion.1), channel_id=1, replica_groups=mesh['visit'=32,'tile'=8] {'visit'}, dimensions={0}, use_global_device_ids=true | all-gather | bytes 270336 | tf_op jit(solution)/shard_map/all_gather | solution.py:73
  439.9 3.8 collective-permute-start.4
  443.7 2.0 collective-permute-start.5
  445.7 3.6 collective-permute-done.5
  449.3 11.2 %fusion.8 = f32[286,31,256]{2,0,1:T(8,128)S(1)} fusion(f32[256,31,256]{0,2,1:T(8,128)} %copy.7, f32[15,256]{1,0:T(8,128)S(1)} %collective-permute-done.5, f32[256,256]{1,0:T(8,128)S(1)} %all_gather.7, f32[15,256]{1,0:T(8,128)S(1)} %collective-permute-done.4), kind=kOutput, calls=%fused_computation.9 | convolution fusion | flops 6972652544 | bytes 17498112 | tf_op jit(solution)/shard_map/dot_general | solution.py:40
  460.5 0.8 fusion.50
  461.3 3.7 collective-permute-start.6
  465.0 2.4 collective-permute-start.7
  467.4 9.2 %collective-permute-done.7 = f32[1,15,256]{2,1,0:T(8,128)S(1)} collective-permute-done((f32[1,15,256]{2,1,0:T(8,128)S(1)}, f32[1,15,256]{2,1,0:T(8,128)S(1)}, u32[]{:S(2)}, u32[]{:S(2)}) %collective-permute-start.7) | collective-permute-done | bytes 15392 | tf_op jit(solution)/shard_map/ppermute | solution.py:17
  476.6 11.2 %fusion.4 = f32[286,31,256]{2,0,1:T(8,128)S(1)} fusion(f32[256,31,256]{0,2,1:T(8,128)} %copy.8, f32[1,15,256]{2,1,0:T(8,128)S(1)} %collective-permute-done.7, f32[1,256,256]{2,1,0:T(8,128)S(1)} %fusion.50, f32[1,15,256]{2,1,0:T(8,128)S(1)} %collective-permute-done.6), kind=kOutput, calls=%fused_computation.5 | convolution fusion | flops 6972652544 | bytes 17498112 | tf_op jit(solution)/shard_map/dot_general | solution.py:40
  487.8 1.4 fusion.34
  489.3 145.9 %reduce-scatter.8.cloned.1.call-done = f32[8,256]{1,0:T(8,128)} async-done(((f32[256,256]{1,0:T(8,128)}), f32[8,256]{1,0:T(8,128)}) %reduce-scatter.8.cloned.1.call-update) | async-done | bytes 8208 | tf_op jit(solution)/shard_map/reduce_scatter | solution.py:82
  635.2 1.3 multiply_divide_fusion
  (31 shorter events, 1.6 us)
Async XLA Ops:
  6.5 249.8 %reduce-scatter.6.cloned.1.call-start = ((), (), s32[]{:S(2)}) async-start(), calls=%async_computation.4 | async-start | bytes 270336 | tf_op jit(solution)/shard_map/reduce_scatter | solution.py:70
  52.1 32.4 %collective-permute-start = (f32[15,256]{1,0:T(8,128)S(1)}, f32[15,256]{1,0:T(8,128)S(1)}, u32[]{:S(2)}, u32[]{:S(2)}) collective-permute-start(f32[15,256]{1,0:T(8,128)S(1)} %get-tuple-element.11), channel_id=1, source_target_pairs={{0,1},{1,2},{2,3},{3,4},{4,5},{5,6},{6,7},{8,9},{9,10},{10,11},{11... | collective-permute-start | bytes 46088 | tf_op jit(solution)/shard_map/ppermute | solution.py:16
  55.5 29.0 %collective-permute-start.1 = (f32[15,256]{1,0:T(8,128)S(1)}, f32[15,256]{1,0:T(8,128)S(1)}, u32[]{:S(2)}, u32[]{:S(2)}) collective-permute-start(f32[15,256]{1,0:T(8,128)S(1)} %get-tuple-element.12), channel_id=1, source_target_pairs={{1,0},{2,1},{3,2},{4,3},{5,4},{6,5},{7,6},{9,8},{10,9},{11,10},{12... | collective-permute-start | bytes 46088 | tf_op jit(solution)/shard_map/ppermute | solution.py:17
  84.4 11.3 %copy-start = (f32[1,256,256]{2,1,0:T(8,128)S(1)}, f32[1,256,256]{2,1,0:T(8,128)}, u32[]{:S(2)}) copy-start(f32[1,256,256]{2,1,0:T(8,128)} %param.4) | copy-start | bytes 786436
  96.5 17.1 %collective-permute-start.2 = (f32[1,15,256]{2,1,0:T(8,128)S(1)}, f32[1,15,256]{2,1,0:T(8,128)S(1)}, u32[]{:S(2)}, u32[]{:S(2)}) collective-permute-start(f32[1,15,256]{2,1,0:T(8,128)S(1)} %get-tuple-element.9), channel_id=1, source_target_pairs={{0,1},{1,2},{2,3},{3,4},{4,5},{5,6},{6,7},{8,9},{9,10},{10,11},{11... | collective-permute-start | bytes 46088 | tf_op jit(solution)/shard_map/ppermute | solution.py:16
  99.9 13.7 %collective-permute-start.3 = (f32[1,15,256]{2,1,0:T(8,128)S(1)}, f32[1,15,256]{2,1,0:T(8,128)S(1)}, u32[]{:S(2)}, u32[]{:S(2)}) collective-permute-start(f32[1,15,256]{2,1,0:T(8,128)S(1)} %get-tuple-element.10), channel_id=1, source_target_pairs={{1,0},{2,1},{3,2},{4,3},{5,4},{6,5},{7,6},{9,8},{10,9},{11,10},{12... | collective-permute-start | bytes 46088 | tf_op jit(solution)/shard_map/ppermute | solution.py:17
  103.5 297.4 %reduce-scatter.4.cloned.1.call-start = ((), (), s32[]{:S(2)}) async-start(), calls=%async_computation.3 | async-start | bytes 270336 | tf_op jit(solution)/shard_map/reduce_scatter | solution.py:82
  124.9 276.0 %copy-start.1 = (f32[8,256]{1,0:T(8,128)S(1)}, f32[8,256]{1,0:T(8,128)}, u32[]{:S(2)}) copy-start(f32[8,256]{1,0:T(8,128)} %param.5) | copy-start | bytes 24580
  126.3 508.8 %reduce-scatter.8.cloned.1.call-start = ((), (), s32[]{:S(2)}) async-start(), calls=%async_computation.5 | async-start | bytes 270336 | tf_op jit(solution)/shard_map/reduce_scatter | solution.py:82
  439.9 5.8 collective-permute-start.4
  443.7 5.6 collective-permute-start.5
  461.3 6.1 collective-permute-start.6
  465.0 11.6 %collective-permute-start.7 = (f32[1,15,256]{2,1,0:T(8,128)S(1)}, f32[1,15,256]{2,1,0:T(8,128)S(1)}, u32[]{:S(2)}, u32[]{:S(2)}) collective-permute-start(f32[1,15,256]{2,1,0:T(8,128)S(1)} %get-tuple-element.6), channel_id=1, source_target_pairs={{1,0},{2,1},{3,2},{4,3},{5,4},{6,5},{7,6},{9,8},{10,9},{11,10},{12... | collective-permute-start | bytes 46088 | tf_op jit(solution)/shard_map/ppermute | solution.py:17
  487.8 147.3 %copy-start.2 = (f32[8,256]{1,0:T(8,128)S(1)}, f32[8,256]{1,0:T(8,128)}, u32[]{:S(2)}) copy-start(f32[8,256]{1,0:T(8,128)} %reduce-scatter.6.cloned.1.call-done) | copy-start | bytes 24580
Sparse Core Ops, SparseCore 0:
  103.7 152.6 reduce-scatter.5
  258.9 141.9 reduce-scatter.3
  489.4 145.6 reduce-scatter.7
where the time goes:
time: 644 us; the launch traced here: 643 us
  waiting for transfers between devices  433 us (67%)
  blocking collectives  83.8 us (13%)
  matrix products  59.2 us (9%)
  starting transfers between devices  23.8 us (4%)
  local copies, waits for them, and re-layouts  20.3 us (3%)
  between operations  13.3 us (2%)
  other arithmetic  9.28 us (1%)
    reduce_scatter x2, waiting for transfers between devices, body(): lax.psum_scatter(numerator, 'visit', scatter_dimension=0, tiled=True)  290 us
    reduce_scatter x1, waiting for transfers between devices, body(): lax.psum_scatter(norm_local, 'visit', scatter_dimension=0, tiled=True)  130 us
    all_gather x2, blocking collectives, body(): whole = lax.all_gather(model_shard, 'visit', axis=0, tiled=True)  83.8 us
    dot_general x4, matrix products, correlate(): product = jnp.dot(extended, operator, precision=lax.Precision.HIGHEST)  44.8 us
    transpose x2, local copies, waits for them, and re-layouts, column_operator(): operator = operator.reshape(width, width, kernel_len).transpose(0, 2, 1)  19.9 us
    ppermute x4, starting transfers between devices, padded(): before = lax.ppermute(last, axis, up)  14.3 us
  transfers between devices with their start and end apart: 11, of which 5 were waited for; matrix products, arithmetic and copies ran while one was open for 8% of the time, Pallas kernels for 0%

commit v1 on v0

--- a/solution.py
+++ b/solution.py
@@ -70,7 +70,10 @@
     norm_shard = lax.psum_scatter(norm_local, "visit", scatter_dimension=0, tiled=True)
     model_shard = sky_model
     for step in range(ITERS):
-        whole = lax.all_gather(model_shard, "visit", axis=0, tiled=True)
+        n_dev = lax.axis_size("visit")
+        blocks = jnp.stack([model_shard for _ in range(n_dev)])
+        blocks = lax.all_to_all(blocks, "visit", split_axis=0, concat_axis=0)
+        whole = jnp.concatenate(blocks, axis=0)
         model_wide = padded(whole, (("tile", 0),), radius)
         member = 0
         blurred = correlate(model_wide, flipped_ops[member])

time: 644 us -> 587 us (0.911)
  blocking collectives: 83.8 us -> 14.3 us
  starting transfers between devices: 23.8 us -> 34.6 us
    all_gather x2 -> x0, blocking collectives: 83.8 us -> none  [body(): whole = lax.all_gather(model_shard, 'visit', axis=0, tiled=True)]
    all_to_all x0 -> x1, blocking collectives: none -> 14.3 us  [body(): blocks = lax.all_to_all(blocks, 'visit', split_axis=0, concat_axis=0)]
    all_to_all x0 -> x1, starting transfers between devices: none -> 8.92 us  [body(): blocks = lax.all_to_all(blocks, 'visit', split_axis=0, concat_axis=0)]
  transfers between devices with their start and end apart: 11 -> 12, of which waited for: 5 -> 5; matrix products, arithmetic and copies ran while one was open for 8% -> 9% of each run, Pallas kernels for 0% -> 0%
where the time goes in v1:
time: 587 us; the launch traced here: 586 us
  waiting for transfers between devices  436 us (74%)
  matrix products  57 us (10%)
  starting transfers between devices  34.6 us (6%)
  local copies, waits for them, and re-layouts  21.7 us (4%)
  blocking collectives  14.3 us (2%)
  between operations  13.4 us (2%)
  other arithmetic  9.25 us (2%)
    reduce_scatter x2, waiting for transfers between devices, body(): lax.psum_scatter(numerator, 'visit', scatter_dimension=0, tiled=True)  290 us
    reduce_scatter x1, waiting for transfers between devices, body(): lax.psum_scatter(norm_local, 'visit', scatter_dimension=0, tiled=True)  133 us
    dot_general x4, matrix products, correlate(): product = jnp.dot(extended, operator, precision=lax.Precision.HIGHEST)  42.5 us
    transpose x2, local copies, waits for them, and re-layouts, column_operator(): operator = operator.reshape(width, width, kernel_len).transpose(0, 2, 1)  19.8 us
    ppermute x4, starting transfers between devices, padded(): before = lax.ppermute(last, axis, up)  15.6 us
    all_to_all x1, blocking collectives, body(): blocks = lax.all_to_all(blocks, 'visit', split_axis=0, concat_axis=0)  14.3 us
    ppermute x4, waiting for transfers between devices, padded(): after = lax.ppermute(initial, axis, down)  12.7 us
    dot_general x2, matrix products, column_operator(): operator = jnp.dot(band_table, kernel.T, precision=lax.Precision.HIGHEST)  12.4 us
  transfers between devices with their start and end apart: 12, of which 5 were waited for; matrix products, arithmetic and copies ran while one was open for 9% of the time, Pallas kernels for 0%

profile of v1, /device:TPU:2, one launch (start us, length us, event | category | flops | bytes accessed | tf_op | source)
XLA Modules:
  0.0 586.4 jit_solution(15270421899262981177)
XLA Ops:
  6.5 1.4 stack.68
  7.9 8.9 %all-to-all-start = ((f32[32,8,256]{2,1,0:T(8,128)}), f32[32,8,256]{2,1,0:T(8,128)S(1)}, u32[]{:S(2)}, u32[]{:S(2)}) async-start(f32[32,8,256]{2,1,0:T(8,128)} %stack.68), calls=%async_computation | async-start | bytes 524288 | tf_op jit(solution)/shard_map/all_to_all | solution.py:75
  17.0 1.4 reduce_sum.18
  18.3 1.4 broadcast_divide_fusion
  19.7 0.9 fusion.116
  20.6 6.3 %fusion.117 = (f32[31,256]{1,0:T(8,128)S(1)}, f32[256,31,256]{2,1,0:T(8,128)}) fusion(f32[1,31,31]{2,0,1:T(1,128)S(1)} %broadcast_divide_fusion, s32[256,256]{1,0:T(8,128)S(1)} %subtract_add_fusion), kind=kOutput, calls=%fused_computation.252 | convolution fusion | flops 759816448 | bytes 8424196 | tf_op jit(solution)/shard_map/dot_general | solution.py:31
  27.1 6.1 %fusion.17 = f32[256,31,256]{2,1,0:T(8,128)} fusion(s32[256,256]{1,0:T(8,128)S(1)} %subtract_add_fusion, f32[31,31]{1,0:T(8,128)S(1)} %rev.3), kind=kOutput, calls=%fused_computation.16 | convolution fusion | flops 757792768 | bytes 8392452 | tf_op jit(solution)/shard_map/dot_general | solution.py:31
  33.3 3.4 collective-permute-start
  36.7 2.4 collective-permute-start.1
  39.3 9.9 %copy.7 = f32[256,31,256]{0,2,1:T(8,128)} copy(f32[256,31,256]{2,1,0:T(8,128)} %fusion.17) | data formatting | bytes 16252928 | tf_op jit(solution)/shard_map/transpose | solution.py:32
  49.3 11.2 %fusion.10 = f32[286,31,256]{2,0,1:T(8,128)S(1)} fusion(f32[256,31,256]{0,2,1:T(8,128)} %copy.7, f32[15,256]{1,0:T(8,128)S(1)} %collective-permute-done.1, f32[256,256]{1,0:T(8,128)S(1)} %bitcast.447, f32[15,256]{1,0:T(8,128)S(1)} %collective-permute-done), kind=kOutput, calls=%fused_computation.11 | convolution fusion | flops 6972652544 | bytes 17498112 | tf_op jit(solution)/shard_map/dot_general | solution.py:40
  60.6 0.8 fusion.81
  61.4 3.4 collective-permute-start.2
  64.8 2.4 collective-permute-start.3
  67.2 1.1 fusion.118
  68.6 9.9 %copy.8 = f32[256,31,256]{0,2,1:T(8,128)} copy(f32[256,31,256]{2,1,0:T(8,128)} %get-tuple-element.47) | data formatting | bytes 16252928 | tf_op jit(solution)/shard_map/transpose | solution.py:32
  78.5 11.2 %fusion.6 = f32[286,31,256]{2,0,1:T(8,128)S(1)} fusion(f32[256,31,256]{0,2,1:T(8,128)} %copy.8, f32[1,15,256]{2,1,0:T(8,128)S(1)} %collective-permute-done.3, f32[1,256,256]{2,1,0:T(8,128)S(1)} %fusion.81, f32[1,15,256]{2,1,0:T(8,128)S(1)} %collective-permute-done.2), kind=kOutput, calls=%fused_computation.7 | convolution fusion | flops 6972652544 | bytes 17498112 | tf_op jit(solution)/shard_map/dot_general | solution.py:40
  89.7 1.4 fusion.65
  91.2 133.2 %reduce-scatter.6.cloned.1.call-done = f32[8,256]{1,0:T(8,128)} async-done(((f32[256,256]{1,0:T(8,128)}), f32[8,256]{1,0:T(8,128)}) %reduce-scatter.6.cloned.1.call-update) | async-done | bytes 8208 | tf_op jit(solution)/shard_map/reduce_scatter | solution.py:70
  224.4 144.2 %reduce-scatter.4.cloned.1.call-done = f32[8,256]{1,0:T(8,128)} async-done(((f32[256,256]{1,0:T(8,128)}), f32[8,256]{1,0:T(8,128)}) %reduce-scatter.4.cloned.1.call-update) | async-done | bytes 8208 | tf_op jit(solution)/shard_map/reduce_scatter | solution.py:85
  369.5 14.3 %all_to_all.10 = f32[32,8,256]{2,1,0:T(8,128)S(1)} all-to-all(f32[32,8,256]{2,1,0:T(8,128)S(1)} %stack.201), channel_id=1, replica_groups=mesh['visit'=32,'tile'=8] {'visit'}, dimensions={0} | all-to-all | bytes 524288 | tf_op jit(solution)/shard_map/all_to_all | solution.py:75
  383.8 3.4 collective-permute-start.4
  387.2 2.7 collective-permute-start.5
  389.9 3.2 collective-permute-done.5
  393.1 11.2 %fusion.8 = f32[286,31,256]{2,0,1:T(8,128)S(1)} fusion(f32[256,31,256]{0,2,1:T(8,128)} %copy.7, f32[15,256]{1,0:T(8,128)S(1)} %collective-permute-done.5, f32[256,256]{1,0:T(8,128)S(1)} %bitcast.449, f32[15,256]{1,0:T(8,128)S(1)} %collective-permute-done.4), kind=kOutput, calls=%fused_computation.9 | convolution fusion | flops 6972652544 | bytes 17498112 | tf_op jit(solution)/shard_map/dot_general | solution.py:40
  405.1 5.4 collective-permute-start.6
  410.5 2.1 collective-permute-start.7
  412.6 9.5 %collective-permute-done.7 = f32[1,15,256]{2,1,0:T(8,128)S(1)} collective-permute-done((f32[1,15,256]{2,1,0:T(8,128)S(1)}, f32[1,15,256]{2,1,0:T(8,128)S(1)}, u32[]{:S(2)}, u32[]{:S(2)}) %collective-permute-start.7) | collective-permute-done | bytes 15392 | tf_op jit(solution)/shard_map/ppermute | solution.py:17
  422.1 8.9 %fusion.4 = f32[286,31,256]{2,0,1:T(8,128)S(1)} fusion(f32[256,31,256]{0,2,1:T(8,128)S(1)} %bitcast.445, f32[1,15,256]{2,1,0:T(8,128)S(1)} %collective-permute-done.7, f32[1,256,256]{2,1,0:T(8,128)S(1)} %fusion.50, f32[1,15,256]{2,1,0:T(8,128)S(1)} %collective-permute-done.6), kind=kOutput, calls=%fused_computation.5 | convolution fusion | flops 6972652544 | bytes 17498112 | tf_op jit(solution)/shard_map/dot_general | solution.py:40
  431.1 1.4 fusion.34
  432.5 146.0 %reduce-scatter.8.cloned.1.call-done = f32[8,256]{1,0:T(8,128)} async-done(((f32[256,256]{1,0:T(8,128)}), f32[8,256]{1,0:T(8,128)}) %reduce-scatter.8.cloned.1.call-update) | async-done | bytes 8208 | tf_op jit(solution)/shard_map/reduce_scatter | solution.py:85
  578.5 1.3 multiply_divide_fusion
  (39 shorter events, 2.4 us)
Async XLA Ops:
  7.9 25.3 %all-to-all-start = ((f32[32,8,256]{2,1,0:T(8,128)}), f32[32,8,256]{2,1,0:T(8,128)S(1)}, u32[]{:S(2)}, u32[]{:S(2)}) async-start(f32[32,8,256]{2,1,0:T(8,128)} %stack.68), calls=%async_computation | async-start | bytes 524288 | tf_op jit(solution)/shard_map/all_to_all | solution.py:75
  16.9 207.6 %reduce-scatter.6.cloned.1.call-start = ((), (), s32[]{:S(2)}) async-start(), calls=%async_computation.6 | async-start | bytes 270336 | tf_op jit(solution)/shard_map/reduce_scatter | solution.py:70
  33.3 16.0 %collective-permute-start = (f32[15,256]{1,0:T(8,128)S(1)}, f32[15,256]{1,0:T(8,128)S(1)}, u32[]{:S(2)}, u32[]{:S(2)}) collective-permute-start(f32[15,256]{1,0:T(8,128)S(1)} %get-tuple-element.11), channel_id=1, source_target_pairs={{0,1},{1,2},{2,3},{3,4},{4,5},{5,6},{6,7},{8,9},{9,10},{10,11},{11... | collective-permute-start | bytes 46088 | tf_op jit(solution)/shard_map/ppermute | solution.py:16
  36.7 12.6 %collective-permute-start.1 = (f32[15,256]{1,0:T(8,128)S(1)}, f32[15,256]{1,0:T(8,128)S(1)}, u32[]{:S(2)}, u32[]{:S(2)}) collective-permute-start(f32[15,256]{1,0:T(8,128)S(1)} %get-tuple-element.12), channel_id=1, source_target_pairs={{1,0},{2,1},{3,2},{4,3},{5,4},{6,5},{7,6},{9,8},{10,9},{11,10},{12... | collective-permute-start | bytes 46088 | tf_op jit(solution)/shard_map/ppermute | solution.py:17
  49.3 11.3 %copy-start = (f32[1,256,256]{2,1,0:T(8,128)S(1)}, f32[1,256,256]{2,1,0:T(8,128)}, u32[]{:S(2)}) copy-start(f32[1,256,256]{2,1,0:T(8,128)} %param.4) | copy-start | bytes 786436
  61.4 17.1 %collective-permute-start.2 = (f32[1,15,256]{2,1,0:T(8,128)S(1)}, f32[1,15,256]{2,1,0:T(8,128)S(1)}, u32[]{:S(2)}, u32[]{:S(2)}) collective-permute-start(f32[1,15,256]{2,1,0:T(8,128)S(1)} %get-tuple-element.9), channel_id=1, source_target_pairs={{0,1},{1,2},{2,3},{3,4},{4,5},{5,6},{6,7},{8,9},{9,10},{10,11},{11... | collective-permute-start | bytes 46088 | tf_op jit(solution)/shard_map/ppermute | solution.py:16
  64.8 13.7 %collective-permute-start.3 = (f32[1,15,256]{2,1,0:T(8,128)S(1)}, f32[1,15,256]{2,1,0:T(8,128)S(1)}, u32[]{:S(2)}, u32[]{:S(2)}) collective-permute-start(f32[1,15,256]{2,1,0:T(8,128)S(1)} %get-tuple-element.10), channel_id=1, source_target_pairs={{1,0},{2,1},{3,2},{4,3},{5,4},{6,5},{7,6},{9,8},{10,9},{11,10},{12... | collective-permute-start | bytes 46088 | tf_op jit(solution)/shard_map/ppermute | solution.py:17
  68.4 300.3 %reduce-scatter.4.cloned.1.call-start = ((), (), s32[]{:S(2)}) async-start(), calls=%async_computation.5 | async-start | bytes 270336 | tf_op jit(solution)/shard_map/reduce_scatter | solution.py:85
  89.7 279.0 %copy-start.1 = (f32[8,256]{1,0:T(8,128)S(1)}, f32[8,256]{1,0:T(8,128)}, u32[]{:S(2)}) copy-start(f32[8,256]{1,0:T(8,128)} %param.5) | copy-start | bytes 24580
  91.2 487.4 %reduce-scatter.8.cloned.1.call-start = ((), (), s32[]{:S(2)}) async-start(), calls=%async_computation.7 | async-start | bytes 270336 | tf_op jit(solution)/shard_map/reduce_scatter | solution.py:85
  369.4 52.7 %slice-start = ((s8[8126464]{0:T(1024)(128)(4,1)}), s8[4194304]{0:T(1024)(128)(4,1)S(1)}, s32[]{:S(2)}) async-start(s8[8126464]{0:T(1024)(128)(4,1)} %bitcast.444), calls=%async_computation.8 | async-start | bytes 8388608
  383.8 6.1 %collective-permute-start.4 = (f32[15,256]{1,0:T(8,128)S(1)}, f32[15,256]{1,0:T(8,128)S(1)}, u32[]{:S(2)}, u32[]{:S(2)}) collective-permute-start(f32[15,256]{1,0:T(8,128)S(1)} %get-tuple-element.7), channel_id=1, source_target_pairs={{0,1},{1,2},{2,3},{3,4},{4,5},{5,6},{6,7},{8,9},{9,10},{10,11},{11... | collective-permute-start | bytes 46088 | tf_op jit(solution)/shard_map/ppermute | solution.py:16
  387.2 35.0 %slice-start.1 = ((s8[8126464]{0:T(1024)(128)(4,1)}), s8[3932160]{0:T(1024)(128)(4,1)S(1)}, s32[]{:S(2)}) async-start(s8[8126464]{0:T(1024)(128)(4,1)} %bitcast.444), calls=%async_computation.9 | async-start | bytes 7864320
  387.2 5.9 %collective-permute-start.5 = (f32[15,256]{1,0:T(8,128)S(1)}, f32[15,256]{1,0:T(8,128)S(1)}, u32[]{:S(2)}, u32[]{:S(2)}) collective-permute-start(f32[15,256]{1,0:T(8,128)S(1)} %get-tuple-element.8), channel_id=1, source_target_pairs={{1,0},{2,1},{3,2},{4,3},{5,4},{6,5},{7,6},{9,8},{10,9},{11,10},{12... | collective-permute-start | bytes 46088 | tf_op jit(solution)/shard_map/ppermute | solution.py:17
  405.1 7.6 %collective-permute-start.6 = (f32[1,15,256]{2,1,0:T(8,128)S(1)}, f32[1,15,256]{2,1,0:T(8,128)S(1)}, u32[]{:S(2)}, u32[]{:S(2)}) collective-permute-start(f32[1,15,256]{2,1,0:T(8,128)S(1)} %get-tuple-element.5), channel_id=1, source_target_pairs={{0,1},{1,2},{2,3},{3,4},{4,5},{5,6},{6,7},{8,9},{9,10},{10,11},{11... | collective-permute-start | bytes 46088 | tf_op jit(solution)/shard_map/ppermute | solution.py:16
  410.5 11.7 %collective-permute-start.7 = (f32[1,15,256]{2,1,0:T(8,128)S(1)}, f32[1,15,256]{2,1,0:T(8,128)S(1)}, u32[]{:S(2)}, u32[]{:S(2)}) collective-permute-start(f32[1,15,256]{2,1,0:T(8,128)S(1)} %get-tuple-element.6), channel_id=1, source_target_pairs={{1,0},{2,1},{3,2},{4,3},{5,4},{6,5},{7,6},{9,8},{10,9},{11,10},{12... | collective-permute-start | bytes 46088 | tf_op jit(solution)/shard_map/ppermute | solution.py:17
  431.1 147.5 %copy-start.2 = (f32[8,256]{1,0:T(8,128)S(1)}, f32[8,256]{1,0:T(8,128)}, u32[]{:S(2)}) copy-start(f32[8,256]{1,0:T(8,128)} %reduce-scatter.6.cloned.1.call-done) | copy-start | bytes 24580
Sparse Core Ops, SparseCore 0:
  68.5 155.8 reduce-scatter.5
  226.9 141.7 reduce-scatter.3
  432.7 145.8 reduce-scatter.7
